TPU v7x, 512 devices: a whole 4x4x16 slice. The times are simulated.
512 devices in a mesh: replica: 64 (over y, z_lo, core), tensor: 8 (over z_hi, x).
Axes of the slice: x: 4, y: 4, z: 16 (z_hi: 2, z_lo: 8; z = z_hi * 8 + z_lo), core: 2. Of those that a mesh axis runs over, the one named last changes fastest.
Arguments:
- hidden_act: bfloat16 [16384, 7168], P('replica', 'tensor'), may hold values from -15 to 15
- residual_in: bfloat16 [512, 65536], P('tensor', 'replica'), may hold values from -6 to 6
- cotangent: bfloat16 [512, 65536], P('tensor', 'replica'), may hold values from -6 to 6
- norm_gain: bfloat16 [2048], replicated, may hold values from 0.25 to 1.75
- inner_weight: bfloat16 [7168, 65536], P('tensor', 'replica'), may hold values from -24 to 24
- anchor: bfloat16 [7168, 2048], P('tensor', 'replica'), may hold values from -6 to 6
- momentum: bfloat16 [7168, 2048], P('tensor', 'replica'), may hold values from -3 to 3
Outputs:
- normed: bfloat16 [512, 65536], P('tensor', 'replica')
- mixed_weight: bfloat16 [7168, 65536], P('tensor', 'replica')
- momentum_out: bfloat16 [7168, 2048], P('tensor', 'replica')
All inputs are finite; a program needn't handle non-finite values.
Results may differ from a plain program's by a relative error of at most 0.0075.
Values may be sent and summed in bfloat16 or wider, within the bound.
A program may use at most 64 MiB of HBM per device.

v0:
```python
import math

import jax
import jax.numpy as jnp
from jax import lax
from jax.sharding import PartitionSpec as P

FF = 7168
TOK = 512


inner_rate = 0.2
outer_rate = 0.7
outer_mu = 0.9
mix_share = 0.5


def partner(array, axis, stride):
    return lax.ppermute(array, axis, [(i, i ^ 1 << stride) for i in range(lax.axis_size(axis))])


def norm_rows(out_rows, resid_rows, cot_rows, norm_scale, total_features):
    summed_in = resid_rows.astype(jnp.float32) + out_rows
    dz_rows = cot_rows.astype(jnp.float32) * norm_scale
    own_squares = jnp.sum(summed_in * summed_in, axis=-1)
    own_cross = jnp.sum(dz_rows * summed_in, axis=-1)
    other_squares, other_cross = partner((own_squares, own_cross), "replica", 0)
    mean_squares = ((own_squares + other_squares) / total_features)[:, None]
    inner_mean = ((own_cross + other_cross) / total_features)[:, None]
    root_inv = lax.rsqrt(mean_squares + 1e-05)
    normed = (summed_in * root_inv * norm_scale).astype(jnp.bfloat16)
    slopes = (root_inv * (dz_rows - summed_in * inner_mean * root_inv * root_inv)).astype(
        jnp.bfloat16
    )
    return (normed, slopes)


def local(hidden_act, residual_in, cotangent, norm_gain, inner_weight, anchor, momentum):
    ff_local = inner_weight.shape[0]
    half_cols = inner_weight.shape[1]
    total_features = 2 * half_cols
    multiplier = 1.0 / math.sqrt(FF)
    step_scale = inner_rate * math.sqrt(FF / TOK)
    side = lax.axis_index("replica") % 2
    first = side == 0
    norm_scale = lax.dynamic_slice_in_dim(norm_gain, side * half_cols, half_cols, 0).astype(
        jnp.float32
    )
    partner_rows = partner(hidden_act, "replica", 0)
    hidden_full = jnp.where(
        first,
        jnp.concatenate([hidden_act, partner_rows], 0),
        jnp.concatenate([partner_rows, hidden_act], 0),
    )
    contract = (((0,), (0,)), ((), ()))
    row_block = hidden_full
    out_rows = lax.psum_scatter(
        jnp.dot(row_block, inner_weight, preferred_element_type=jnp.float32) * multiplier,
        "tensor",
        scatter_dimension=0,
        tiled=True,
    )
    normed, slopes = norm_rows(out_rows, residual_in, cotangent, norm_scale, total_features)
    row_block = hidden_full
    gradient = lax.dot_general(
        row_block,
        lax.all_gather(slopes, "tensor", axis=0, tiled=True),
        contract,
        preferred_element_type=jnp.float32,
    )
    gradient = gradient * multiplier
    stepped = inner_weight.astype(jnp.float32) - step_scale * gradient
    replica_count = lax.axis_size("replica") // 2
    buffer = jnp.zeros((1, ff_local, total_features), jnp.bfloat16)
    buffer = lax.dynamic_update_slice(buffer, inner_weight[None], (0, 0, side * half_cols))
    received = lax.all_to_all(buffer, "replica", split_axis=2, concat_axis=0, tiled=True)
    summed = jnp.sum(received, axis=0, dtype=jnp.float32)
    anchor_f = anchor.astype(jnp.float32)
    pseudo = anchor_f - summed / replica_count
    moment = (outer_mu * momentum.astype(jnp.float32) + pseudo).astype(jnp.bfloat16)
    new_anchor = (anchor_f - outer_rate * (pseudo + outer_mu * moment.astype(jnp.float32))).astype(
        jnp.bfloat16
    )
    full_anchor = lax.all_gather(new_anchor, "replica", axis=1, tiled=True)
    own_anchor = lax.dynamic_slice_in_dim(full_anchor, side * half_cols, half_cols, 1)
    mixed = (mix_share * stepped + (1.0 - mix_share) * own_anchor.astype(jnp.float32)).astype(
        jnp.bfloat16
    )
    return (normed, mixed, moment)


def solution(mesh):
    in_specs = (
        P("replica", "tensor"),
        P("tensor", "replica"),
        P("tensor", "replica"),
        P(),
        P("tensor", "replica"),
        P("tensor", "replica"),
        P("tensor", "replica"),
    )
    out_specs = (P("tensor", "replica"), P("tensor", "replica"), P("tensor", "replica"))
    return jax.shard_map(local, mesh=mesh, in_specs=in_specs, out_specs=out_specs, check_vma=False)
```

profile of v0, /device:TPU:24, one launch (start us, length us, event | category | flops | bytes accessed | tf_op | source)
XLA Modules:
  0.0 599.6 jit_solution(8487567397777229452)
XLA Ops:
  8.0 9.8 %copy.20 = bf16[1,896,1024]{1,0,2:T(2,128)(2,1)} copy(bf16[1,896,1024]{2,1,0:T(8,128)(2,1)} %bitcast.9) | data formatting | bytes 3670016 | tf_op jit(solution)/shard_map/broadcast_in_dim | solution.py:75
  17.8 0.0 copy-start
  17.8 4.9 broadcast_in_dim.4
  22.7 0.0 copy-done
  22.7 5.6 constant_dynamic-update-slice_fusion
  28.3 0.5 broadcast.27
  28.8 79.9 %reduce.3 = bf16[2048,896]{1,0:T(8,128)(2,1)} reduce(bf16[2048,1,896]{2,1,0:T(2,128)(2,1)} %bitcast.3, bf16[]{:T(256)} %broadcast.27), dimensions={1}, to_apply=%bitcast.3.reduce_sub_computation | reduce | bytes 7340034
  108.7 8.3 %reshape.16 = bf16[64,2,14336]{2,1,0:T(2,128)(2,1)} reshape(bf16[2048,896]{1,0:T(8,128)(2,1)} %reduce.3) | data formatting | bytes 7340032
  117.0 0.0 copy-start.7
  117.0 16.4 %all-to-all-start = ((bf16[64,2,14336]{2,1,0:T(2,128)(2,1)}), bf16[64,2,14336]{2,1,0:T(2,128)(2,1)}, u32[]{:S(2)}, u32[]{:S(2)}) async-start(bf16[64,2,14336]{2,1,0:T(2,128)(2,1)} %reshape.16), calls=%async_computation.1 | async-start | bytes 7340032 | tf_op jit(solution)/shard_map/all_to_all | solution.py:76
  133.4 0.0 reduce-scatter.2.cloned.1.call-start
  133.5 0.0 copy-done.7
  133.5 2.1 collective-permute-start
  135.6 1.6 collective-permute-done
  137.2 0.0 copy-done.1
  137.2 2.6 convolution_multiply_fusion
  139.8 0.0 reduce-scatter.2.cloned.1.call-update
  139.9 0.0 all-gather.5.cloned.1.call-start
  139.9 210.0 %all-to-all-done = bf16[64,2,14336]{2,1,0:T(2,128)(2,1)} async-done(((bf16[64,2,14336]{2,1,0:T(2,128)(2,1)}), bf16[64,2,14336]{2,1,0:T(2,128)(2,1)}, u32[]{:S(2)}, u32[]{:S(2)}) %all-to-all-start) | async-done | bytes 3670048 | tf_op jit(solution)/shard_map/all_to_all | solution.py:76
  349.9 19.3 %reshape.17 = bf16[2048,1,896]{2,1,0:T(2,128)(2,1)} reshape(bf16[64,2,14336]{2,1,0:T(2,128)(2,1)} %all-to-all-done) | data formatting | bytes 7340032
  369.2 3.7 copy.21
  372.9 0.0 copy-start.4
  372.9 0.0 copy-start.5
  372.9 0.0 copy-start.6
  372.9 0.0 copy-start.2
  372.9 0.0 copy-start.3
  372.9 0.5 convert_reduce_fusion
  373.5 0.2 copy-done.4
  373.7 0.0 copy-done.5
  373.7 0.7 fusion
  374.4 0.0 all-gather.5.cloned.1.call-update
  374.4 0.0 all-gather.3.cloned.1.call-start
  374.5 0.0 copy-done.6
  374.5 0.0 reduce-scatter.2.cloned.1.call-done
  374.5 0.0 copy-done.2
  374.6 0.0 copy-done.3
  374.6 1.1 multiply_reduce_fusion
  375.7 4.9 collective-permute-start.1
  380.6 1.9 collective-permute-start.2
  382.6 0.0 collective-permute-done.1
  382.6 1.1 collective-permute-done.2
  383.7 1.8 multiply_convert_fusion.1
  385.5 0.0 all-gather.3.cloned.1.call-update
  385.5 108.9 %all-gather.5.cloned.1.call-done = bf16[896,2048]{0,1:T(8,128)(2,1)} async-done(((bf16[896,32]{0,1:T(8,128)(2,1)}), bf16[896,2048]{0,1:T(8,128)(2,1)}) %all-gather.5.cloned.1.call-update) | async-done | bytes 3670032 | tf_op jit(solution)/shard_map/all_gather | solution.py:84
  494.4 1.6 constant_dynamic-slice_fusion
  496.1 2.4 copy.23
  498.5 88.6 %all-gather.3.cloned.1.call-done = bf16[512,1024]{1,0:T(8,128)(2,1)} async-done(((bf16[64,1024]{1,0:T(8,128)(2,1)}), bf16[512,1024]{1,0:T(8,128)(2,1)}) %all-gather.3.cloned.1.call-update) | async-done | bytes 1048592 | tf_op jit(solution)/shard_map/all_gather | solution.py:67
  587.0 5.1 multiply_convert_fusion
  (4 shorter events, 0.0 us)
Async XLA Ops:
  17.8 4.9 copy-start
  117.0 16.5 %copy-start.7 = (bf16[256,896]{1,0:T(8,128)(2,1)S(1)}, bf16[256,896]{1,0:T(8,128)(2,1)}, u32[]{:S(2)}) copy-start(bf16[256,896]{1,0:T(8,128)(2,1)} %param.7) | copy-start | bytes 1376260
  117.0 20.2 %copy-start.1 = (bf16[896,1024]{1,0:T(8,128)(2,1)S(1)}, bf16[896,1024]{1,0:T(8,128)(2,1)}, u32[]{:S(2)}) copy-start(bf16[896,1024]{1,0:T(8,128)(2,1)} %param.11) | copy-start | bytes 5505028
  117.0 232.9 %all-to-all-start = ((bf16[64,2,14336]{2,1,0:T(2,128)(2,1)}), bf16[64,2,14336]{2,1,0:T(2,128)(2,1)}, u32[]{:S(2)}, u32[]{:S(2)}) async-start(bf16[64,2,14336]{2,1,0:T(2,128)(2,1)} %reshape.16), calls=%async_computation.1 | async-start | bytes 7340032 | tf_op jit(solution)/shard_map/all_to_all | solution.py:76
  133.4 241.1 %reduce-scatter.2.cloned.1.call-start = ((), (), s32[]{:S(2)}) async-start(), calls=%async_computation.2 | async-start | bytes 2359296 | tf_op jit(solution)/shard_map/reduce_scatter | solution.py:57
  133.5 3.7 collective-permute-start
  139.9 354.5 %all-gather.5.cloned.1.call-start = ((), (), s32[]{:S(2)}) async-start(), calls=%async_computation.4 | async-start | bytes 3727360 | tf_op jit(solution)/shard_map/all_gather | solution.py:84
  372.9 0.8 copy-start.4
  372.9 0.8 copy-start.5
  372.9 1.6 copy-start.6
  372.9 1.6 copy-start.2
  372.9 1.6 copy-start.3
  374.4 212.6 %all-gather.3.cloned.1.call-start = ((), (), s32[]{:S(2)}) async-start(), calls=%async_computation.3 | async-start | bytes 1179648 | tf_op jit(solution)/shard_map/all_gather | solution.py:67
  375.7 6.9 %collective-permute-start.1 = (f32[64]{0:T(128)S(1)}, f32[64]{0:T(128)S(1)}, u32[]{:S(2)}, u32[]{:S(2)}) collective-permute-start(f32[64]{0:T(128)S(1)} %get-tuple-element.10), channel_id=1, source_target_pairs={{0,8},{8,0},{16,24},{24,16},{32,40},{40,32},{48,56},{56,48},{64,72... | collective-permute-start | bytes 776 | tf_op jit(solution)/shard_map/ppermute | solution.py:19
  380.6 3.0 collective-permute-start.2
Sparse Core Ops, SparseCore 0:
  140.0 208.5 reduce-scatter.1
Sparse Core Ops, SparseCore 1:
  374.5 119.8 all-gather.4
  498.0 89.0 all-gather.2
where the time goes:
time: 601 us; the launch traced here: 600 us
  waiting for transfers between devices  410 us (68%)
  other arithmetic  84 us (14%)
  local copies, waits for them, and re-layouts  56.4 us (9%)
  starting transfers between devices  25.5 us (4%)
  between operations  15.7 us (3%)
  matrix products  7.79 us (1%)
    all_to_all x1, waiting for transfers between devices, local(): lax.all_to_all(buffer, 'replica', split_axis=2, concat_axis=0, tiled=True)  210 us
    all_gather x1, waiting for transfers between devices, local(): full_anchor = lax.all_gather(new_anchor, 'replica', axis=1, tiled=True)  109 us
    all_gather x1, waiting for transfers between devices, local(): lax.all_gather(slopes, 'tensor', axis=0, tiled=True)  88.6 us
    unnamed x1, other arithmetic  79.9 us
    unnamed x20, local copies, waits for them, and re-layouts  30.9 us
    all_to_all x1, starting transfers between devices, local(): lax.all_to_all(buffer, 'replica', split_axis=2, concat_axis=0, tiled=True)  16.4 us
  transfers between devices with their start and end apart: 7, of which 5 were waited for; matrix products, arithmetic and copies ran while one was open for 6% of the time, Pallas kernels for 0%

commit v1 on v0

v1 whole, which is shorter than its diff:
```python
import math

import jax
import jax.numpy as jnp
from jax import lax
from jax.experimental import pallas as pl
from jax.experimental.pallas import tpu as pltpu
from jax.sharding import PartitionSpec as P

FF = 7168
TOK = 512

inner_rate = 0.2
outer_rate = 0.7
outer_mu = 0.9
mix_share = 0.5

F32 = jnp.float32
BF16 = jnp.bfloat16
ROWS = 896
COLS = 1024
CHUNKS = ((0, 512), (512, 384))
REPLICAS = 32
FEATURES = 2048
MULT = 1.0 / math.sqrt(FF)
STEP = inner_rate * math.sqrt(FF / TOK)
NSEM = 72


def kernel(
    h_hbm, r_hbm, c_hbm, gain, w_hbm, at_hbm, mt_hbm,
    normed_hbm, mixed_hbm, mout_hbm,
    wv, hb, ht, p32, pb, ap1, ap2, xown, zsend, zrecv, rv, cv, stat_out, stat_in, sb, nout,
    p1buf, cbuf, yrecv, yown, tt, q1r, qs, near, far, atv, mtv, nown, mo, ta, na, nfull,
    base, mix, send, recv, loc,
):
    ri = lax.axis_index("replica")
    ti = lax.axis_index("tensor")
    s = lax.rem(ri, 2)
    chip = lax.div(ri, 2)
    z = lax.rem(chip, 8)
    y = lax.div(chip, 8)
    zh = lax.div(ti, 4)
    x = lax.rem(ti, 4)
    q = lax.div(z, 4)
    p = lax.rem(z, 4)
    zfar = 4 * (1 - q) + p
    o = 1 - s
    sy = lax.div(y, 2)
    je = lax.rem(y, 2)
    jo = 1 - je
    yb = 2 * s + jo
    plus = lax.rem(yb - y + 4, 4) == 1
    hc = jnp.where(plus, 1, 0)
    hd = 1 - hc
    side = 1 - hc
    yo = lax.rem(2 * y - yb + 4, 4)
    yup = lax.rem(y + 1, 4)
    ydn = lax.rem(y + 3, 4)
    xup = lax.rem(x + 1, 4)
    xdn = lax.rem(x + 3, 4)
    xfar = lax.rem(x + 2, 4)
    own = s == sy
    is_near = s == q

    def dev(yy=y, zz=z, cc=s, hh=zh, xx=x):
        return ((yy * 8 + zz) * 2 + cc, hh * 4 + xx)

    ids = {}
    used = {"r": 0, "s": 0}

    def sid(name, count=1):
        if name not in ids:
            kind = "r" if name.startswith("r_") else "s"
            ids[name] = used[kind]
            used[kind] += count
            assert used[kind] <= NSEM
        return ids[name]

    pending = []

    def when(cond, f):
        if cond is None:
            f()
        else:
            pl.when(cond)(f)

    other = dev(cc=o)

    def go(sname, ridx, src, dst, device, cond=None):
        d = pltpu.make_async_remote_copy(
            src_ref=src, dst_ref=dst, send_sem=send.at[sid("s_" + sname)], recv_sem=recv.at[ridx],
            device_id=device, device_id_type=pl.DeviceIdType.MESH,
        )
        when(cond, d.start)
        pending.append((cond, d))

    def got(ridx, dst, cond=None):
        d = pltpu.make_async_remote_copy(
            src_ref=dst, dst_ref=dst, send_sem=send.at[0], recv_sem=recv.at[ridx],
            device_id=other, device_id_type=pl.DeviceIdType.MESH,
        )
        when(cond, d.wait_recv)

    nloc = [0]

    def local_copy(src, dst):
        d = pltpu.make_async_copy(src, dst, loc.at[nloc[0]])
        nloc[0] += 1
        return d

    peers = [other, dev(xx=xup), dev(xx=xdn), dev(hh=1 - zh)]
    for yy in (yup, ydn):
        peers += [dev(yy=yy, cc=0), dev(yy=yy, cc=1)]
    for k in (1, 2, 3):
        peers.append(dev(zz=4 * q + lax.rem(p + k, 4)))
    peers += [dev(zz=zfar, cc=0), dev(zz=zfar, cc=1)]
    lw = local_copy(w_hbm, wv)
    lh = local_copy(h_hbm, hb.at[s])
    lr = local_copy(r_hbm, rv)
    lc = local_copy(c_hbm, cv)
    la = local_copy(at_hbm, atv)
    lm = local_copy(mt_hbm, mtv)
    for d in (lh, lw, lr, lc, la, lm):
        d.start()
    barrier = pltpu.get_barrier_semaphore()
    for peer in peers:
        pl.semaphore_signal(barrier, inc=1, device_id=peer, device_id_type=pl.DeviceIdType.MESH)
    pl.semaphore_wait(barrier, len(peers))

    def lane(value):
        return pl.multiple_of(value, 256)

    def wcols(j, h):
        return pl.ds(lane(j * 512 + h * 256), 256)

    go("h", sid("r_h"), h_hbm, hb.at[s], other)

    own_local = []
    for k, (r0, n) in enumerate(CHUNKS):
        rows = pl.ds(r0, n)
        rp1 = sid(f"r_p1{k}")
        ryo = sid(f"r_yo{k}")
        go(f"p1a{k}", rp1, w_hbm.at[rows, wcols(je, 0)], p1buf.at[rows], dev(yy=ydn), jnp.logical_not(own))
        go(f"p1b{k}", rp1, w_hbm.at[rows, wcols(je, 1)], p1buf.at[rows], dev(yy=yup), jnp.logical_not(own))
        go(f"yo{k}", ryo, w_hbm.at[rows, wcols(je, o)], yown.at[rows], other, own)
        d = local_copy(w_hbm.at[rows, wcols(je, s)], yown.at[rows])
        when(own, d.start)
        own_local.append(d)
    for k, (r0, n) in enumerate(CHUNKS):
        rows = pl.ds(r0, n)
        ryr = sid(f"r_yr{k}", 2)
        go(f"yd{k}", ryr + side, w_hbm.at[rows, wcols(jo, hd)], yrecv.at[side, rows], dev(yy=yb, cc=hd))

    def partial_out(half):
        @pl.loop(0, COLS // 256)
        def _(i):
            cols = pl.ds(lane(i * 256), 256)
            v = jnp.dot(hb[half], wv[:, cols], preferred_element_type=F32).reshape(4, 64, 256)
            p32[half, :, :, cols] = v
            pb[half, :, :, cols] = v.astype(BF16)

    lh.wait()
    lw.wait()
    partial_out(s)
    got(sid("r_h"), hb.at[o])
    partial_out(o)

    halves = (1 - zh, zh)
    for k, hf in enumerate(halves):
        ra = sid(f"r_ap1{k}", 2)
        go(f"ap1a{k}", ra, pb.at[hf, xfar, pl.ds(0, 32)], ap1.at[k, 0], dev(xx=xdn))
        go(f"ap1b{k}", ra + 1, pb.at[hf, xfar, pl.ds(32, 32)], ap1.at[k, 1], dev(xx=xup))

    def combine(k):
        r0, n = CHUNKS[k]
        rows = pl.ds(r0, n)
        got(sid(f"r_p1{k}"), p1buf.at[rows])

        @pl.loop(0, n // 128)
        def _(i):
            t = pl.ds(pl.multiple_of(r0 + i * 128, 128), 128)
            cbuf[t, :] = (wv[t, wcols(jo, hc)].astype(F32) + p1buf[t, :].astype(F32)).astype(BF16)

        go(f"yc{k}", sid(f"r_yr{k}") + side, cbuf.at[rows], yrecv.at[side, rows], dev(yy=yb, cc=hc))

    combine(0)
    combine(1)

    for k, hf in enumerate(halves):
        ra = sid(f"r_ap1{k}")
        rb = sid(f"r_ap2{k}", 2)
        got(ra + 1, ap1.at[k, 1])
        pb[hf, xup, 32:64, :] = (p32[hf, xup, 32:64, :] + ap1[k, 1].astype(F32)).astype(BF16)
        go(f"ap2a{k}", rb, pb.at[hf, xup], ap2.at[k, 0], dev(xx=xup))
        got(ra, ap1.at[k, 0])
        pb[hf, xdn, 0:32, :] = (p32[hf, xdn, 0:32, :] + ap1[k, 0].astype(F32)).astype(BF16)
        go(f"ap2b{k}", rb + 1, pb.at[hf, xdn], ap2.at[k, 1], dev(xx=xdn))

    for hf in range(2):
        @pl.loop(0, ROWS // 128)
        def _(i):
            t = pl.ds(pl.multiple_of(i * 128, 128), 128)
            ht[hf, t, :] = hb[hf, :, t].astype(F32).T.astype(BF16)

    def quad_send(k):
        r0, n = CHUNKS[k]
        rows = pl.ds(r0, n)
        for i in range(2):
            got(sid(f"r_yr{k}") + i, yrecv.at[i, rows])
        got(sid(f"r_yo{k}"), yown.at[rows], jnp.logical_not(own))
        when(own, own_local[k].wait)

        @pl.loop(0, n // 128)
        def _(i):
            t = pl.ds(pl.multiple_of(r0 + i * 128, 128), 128)
            v = yown[t, :].astype(F32) + yrecv[0, t, :].astype(F32) + yrecv[1, t, :].astype(F32)
            tt[:, :, t] = v.T.astype(BF16).reshape(4, 64, 128)

        rq = sid(f"r_q{k}", 3)
        for m in (1, 2, 3):
            pm = lax.rem(p + m, 4)
            go(f"q{k}{m}", rq + m - 1, tt.at[pm, :, rows], q1r.at[m - 1, :, rows], dev(zz=4 * q + pm))

    quad_send(0)

    def finish_out(k):
        hf = halves[k]
        rb = sid(f"r_ap2{k}")
        got(rb, ap2.at[k, 0])
        got(rb + 1, ap2.at[k, 1])
        return p32[hf, x] + ap2[k, 0].astype(F32) + ap2[k, 1].astype(F32)

    zsend[...] = finish_out(0).astype(BF16)
    go("z", sid("r_z"), zsend, zrecv, dev(hh=1 - zh))
    xown[...] = finish_out(1)

    quad_send(1)

    def far_send(k):
        r0, n = CHUNKS[k]
        rows = pl.ds(r0, n)
        rq = sid(f"r_q{k}")
        for m in (1, 2, 3):
            got(rq + m - 1, q1r.at[m - 1, :, rows])
        v = tt[p, :, r0:r0 + n].astype(F32)
        for m in range(3):
            v = v + q1r[m, :, r0:r0 + n].astype(F32)
        qs[:, :, r0:r0 + n] = v.astype(BF16).reshape(2, 32, n)
        rn = sid(f"r_near{k}")
        rf = sid(f"r_far{k}")
        go(f"near{k}", rn, qs.at[o, :, rows], near.at[:, rows], other, is_near)
        for c in range(2):
            go(f"far{k}{c}", rf, qs.at[c, :, rows], far.at[:, rows], dev(zz=zfar, cc=c), jnp.logical_not(is_near))

        @pl.when(is_near)
        def _():
            near[:, r0:r0 + n] = qs[s, :, r0:r0 + n]

    far_send(0)
    far_send(1)

    lr.wait()
    lc.wait()
    got(sid("r_z"), zrecv)
    scale = gain[s]
    xin = rv[...].astype(F32) + (xown[...] + zrecv[...].astype(F32)) * MULT
    dz = cv[...].astype(F32) * scale
    sq = jnp.sum(xin * xin, axis=-1, keepdims=True)
    cr = jnp.sum(dz * xin, axis=-1, keepdims=True)
    xown[...] = xin
    stat_out[0] = jnp.broadcast_to(sq, (64, 128))
    stat_out[1] = jnp.broadcast_to(cr, (64, 128))
    go("stat", sid("r_stat"), stat_out, stat_in, other)
    got(sid("r_stat"), stat_in)
    mean_sq = (stat_out[0, :, 0:1] + stat_in[0, :, 0:1]) / FEATURES
    inner_mean = (stat_out[1, :, 0:1] + stat_in[1, :, 0:1]) / FEATURES
    root_inv = lax.rsqrt(mean_sq + 1e-05)
    xin = xown[...]
    dz = cv[...].astype(F32) * scale
    sb[zh, x] = (root_inv * (dz - xin * (inner_mean * root_inv * root_inv))).astype(BF16)
    go("zs", sid("r_zs"), sb.at[zh, x], sb.at[zh, x], dev(hh=1 - zh))

    def spread(k, hf):
        rs = sid(f"r_s{k}", 4)
        go(f"su{k}", rs, sb.at[hf, x], sb.at[hf, x], dev(xx=xup))
        go(f"sd{k}", rs + 1, sb.at[hf, x], sb.at[hf, x], dev(xx=xdn))

    def relay(k, hf):
        rs = sid(f"r_s{k}")
        got(rs + 1, sb.at[hf, xup])
        go(f"fd{k}", rs + 3, sb.at[hf, xup, pl.ds(32, 32)], sb.at[hf, xup, pl.ds(32, 32)], dev(xx=xdn))
        got(rs, sb.at[hf, xdn])
        go(f"fu{k}", rs + 2, sb.at[hf, xdn, pl.ds(0, 32)], sb.at[hf, xdn, pl.ds(0, 32)], dev(xx=xup))

    def relayed(k, hf):
        rs = sid(f"r_s{k}")
        got(rs + 2, sb.at[hf, xfar, pl.ds(0, 32)])
        got(rs + 3, sb.at[hf, xfar, pl.ds(32, 32)])

    spread(0, zh)
    nout[...] = (xin * root_inv * scale).astype(BF16)
    ln = local_copy(nout, normed_hbm)
    ln.start()

    la.wait()
    lm.wait()

    def update(k):
        r0, n = CHUNKS[k]
        rows = pl.ds(r0, n)
        cut = slice(r0, r0 + n)
        got(sid(f"r_near{k}"), near.at[:, rows], jnp.logical_not(is_near))
        got(sid(f"r_far{k}"), far.at[:, rows])
        total = near[:, cut].astype(F32) + far[:, cut].astype(F32)
        anchor = atv[:, cut].astype(F32)
        pseudo = anchor - total / REPLICAS
        moment = (outer_mu * mtv[:, cut].astype(F32) + pseudo).astype(BF16)
        mo[:, cut] = moment
        fresh = (anchor - outer_rate * (pseudo + outer_mu * moment.astype(F32))).astype(BF16)
        nown[:, cut] = fresh
        rt = sid(f"r_ta{k}", 2)
        go(f"tf{k}", rt + s, nown.at[:, rows], ta.at[p, s, :, rows], dev(zz=zfar, cc=q))
        go(f"tn{k}", rt + s, nown.at[:, rows], ta.at[p, s, :, rows], other, jnp.logical_not(is_near))

        @pl.when(is_near)
        def _():
            ta[p, s, :, cut] = fresh

    update(0)
    update(1)
    lo = local_copy(mo, mout_hbm)
    lo.start()

    def quad_gather(k):
        r0, n = CHUNKS[k]
        rows = pl.ds(r0, n)
        rt = sid(f"r_ta{k}")
        for c in range(2):
            got(rt + c, ta.at[p, c, :, rows], jnp.logical_not(jnp.logical_and(is_near, s == c)))
        rg = sid(f"r_g{k}", 3)
        for m in (1, 2, 3):
            pm = lax.rem(p + m, 4)
            go(f"g{k}{m}", rg + m - 1, ta.at[p, :, :, rows], ta.at[p, :, :, rows], dev(zz=4 * q + pm))

    quad_gather(0)
    quad_gather(1)
    relay(0, zh)

    def row_gather(k):
        r0, n = CHUNKS[k]
        rows = pl.ds(r0, n)
        rg = sid(f"r_g{k}")
        for m in (1, 2, 3):
            got(rg + m - 1, ta.at[lax.rem(p + 4 - m, 4), :, :, rows])

        @pl.loop(0, n // 128)
        def _(i):
            t = pl.ds(pl.multiple_of(r0 + i * 128, 128), 128)
            v = ta[:, :, :, t].reshape(256, 128).astype(F32).T.astype(BF16)
            na[t, :] = v

            @pl.when(own)
            def _():
                nfull[t, wcols(je, s)] = v

        ro = sid(f"r_no{k}", 2)
        re = sid(f"r_ne{k}", 2)
        dst = nfull.at[rows, wcols(je, s)]
        go(f"nu{k}", ro + s, na.at[rows], dst, dev(yy=yup, cc=sy))
        go(f"nd{k}", ro + s, na.at[rows], dst, dev(yy=ydn, cc=sy))
        go(f"nn{k}", re + s, na.at[rows], dst, other, jnp.logical_not(own))

    row_gather(0)
    row_gather(1)

    relayed(0, zh)
    shrink = mix_share * STEP * MULT

    @pl.loop(0, COLS // 256)
    def _(i):
        cols = pl.ds(lane(i * 256), 256)
        g = jnp.dot(ht[zh], sb[zh, :, :, cols].reshape(256, 256), preferred_element_type=F32)
        base[:, cols] = mix_share * wv[:, cols].astype(F32) - shrink * g

    got(sid("r_zs"), sb.at[1 - zh, x])
    spread(1, 1 - zh)

    def row_relay(k):
        r0, n = CHUNKS[k]
        rows = pl.ds(r0, n)
        ro = sid(f"r_no{k}")
        for h in range(2):
            got(ro + h, nfull.at[rows, wcols(jo, h)])
        part = nfull.at[rows, wcols(jo, hc)]
        go(f"nf{k}", sid(f"r_ne{k}") + hc, part, part, dev(yy=yo))

    row_relay(0)
    relay(1, 1 - zh)
    row_relay(1)
    relayed(1, 1 - zh)

    for k, (r0, n) in enumerate(CHUNKS):
        re = sid(f"r_ne{k}")
        for h in range(2):
            got(re + h, nfull.at[pl.ds(r0, n), wcols(je, h)], jnp.logical_not(jnp.logical_and(own, s == h)))

    outs = []
    for i in range(COLS // 256):
        cols = pl.ds(i * 256, 256)
        g = jnp.dot(ht[1 - zh], sb[1 - zh, :, :, cols].reshape(256, 256), preferred_element_type=F32)
        mix[:, cols] = (base[:, cols] - shrink * g + (1.0 - mix_share) * nfull[:, cols].astype(F32)).astype(BF16)
        d = local_copy(mix.at[:, cols], mixed_hbm.at[:, cols])
        d.start()
        outs.append(d)
    for cond, d in pending:
        when(cond, d.wait_send)
    ln.wait()
    lo.wait()
    for d in outs:
        d.wait()


def local(hidden_act, residual_in, cotangent, norm_gain, inner_weight, anchor, momentum):
    hbm = pl.BlockSpec(memory_space=pl.ANY)
    vmem = pl.BlockSpec(memory_space=pltpu.VMEM)
    gain = norm_gain.astype(F32).reshape(2, 1, COLS)
    b16 = lambda *shape: pltpu.VMEM(shape, BF16)
    f32 = lambda *shape: pltpu.VMEM(shape, F32)
    normed, mixed, moment = pl.pallas_call(
        kernel,
        out_shape=(
            jax.ShapeDtypeStruct((64, COLS), BF16),
            jax.ShapeDtypeStruct((ROWS, COLS), BF16),
            jax.ShapeDtypeStruct((32, ROWS), BF16),
        ),
        in_specs=[hbm, hbm, hbm, vmem, hbm, hbm, hbm],
        out_specs=(hbm, hbm, hbm),
        scratch_shapes=[
            b16(ROWS, COLS), b16(2, 256, ROWS), b16(2, ROWS, 256), f32(2, 4, 64, COLS), b16(2, 4, 64, COLS),
            b16(2, 2, 32, COLS), b16(2, 2, 64, COLS), f32(64, COLS), b16(64, COLS), b16(64, COLS),
            b16(64, COLS), b16(64, COLS), f32(2, 64, 128), f32(2, 64, 128), b16(2, 4, 64, COLS), b16(64, COLS),
            b16(ROWS, 256), b16(ROWS, 256), b16(2, ROWS, 256), b16(ROWS, 256), b16(4, 64, ROWS),
            b16(3, 64, ROWS), b16(2, 32, ROWS), b16(32, ROWS), b16(32, ROWS), b16(32, ROWS), b16(32, ROWS),
            b16(32, ROWS), b16(32, ROWS), b16(4, 2, 32, ROWS), b16(ROWS, 256), b16(ROWS, COLS),
            f32(ROWS, COLS), b16(ROWS, COLS),
            pltpu.SemaphoreType.DMA((NSEM,)), pltpu.SemaphoreType.DMA((NSEM,)), pltpu.SemaphoreType.DMA((24,)),
        ],
        compiler_params=pltpu.CompilerParams(
            collective_id=0, has_side_effects=True, vmem_limit_bytes=56 * 1024 * 1024
        ),
    )(hidden_act, residual_in, cotangent, gain, inner_weight, anchor.T, momentum.T)
    return (normed, mixed, moment.T)


def solution(mesh):
    in_specs = (
        P("replica", "tensor"),
        P("tensor", "replica"),
        P("tensor", "replica"),
        P(),
        P("tensor", "replica"),
        P("tensor", "replica"),
        P("tensor", "replica"),
    )
    out_specs = (P("tensor", "replica"), P("tensor", "replica"), P("tensor", "replica"))
    return jax.shard_map(local, mesh=mesh, in_specs=in_specs, out_specs=out_specs, check_vma=False)
```

time: 601 us -> 107 us (0.18)
  waiting for transfers between devices: 410 us -> 0 us
  Pallas kernels: 0 us -> 98.5 us
  other arithmetic: 84 us -> 1.29 us
  local copies, waits for them, and re-layouts: 56.4 us -> 5.07 us
  starting transfers between devices: 25.5 us -> 0 us
  between operations: 15.7 us -> 0.64 us
  matrix products: 7.79 us -> 0 us
    all_to_all x1 -> x0, waiting for transfers between devices: 210 us -> none  [local(): lax.all_to_all(buffer, 'replica', split_axis=2, concat_axis=0, tiled=True)]
    all_gather x2 -> x0, waiting for transfers between devices: 197 us -> none  [the longest x1 109 us: local(): full_anchor = lax.all_gather(new_anchor, 'replica', axis=1, tiled=True)]
    pallas_call x0 -> x1, Pallas kernels: none -> 98.5 us  [local(): pl.pallas_call(kernel, out_shape=(jax.ShapeDtypeStruct((64, COLS), BF16),...]
    unnamed x1 -> x0, other arithmetic: 79.9 us -> none
    unnamed x20 -> x5, local copies, waits for them, and re-layouts: 30.9 us -> 5.07 us
    all_to_all x1 -> x0, starting transfers between devices: 16.4 us -> none  [local(): lax.all_to_all(buffer, 'replica', split_axis=2, concat_axis=0, tiled=True)]
    broadcast_in_dim x2 -> x0, local copies, waits for them, and re-layouts: 14.7 us -> none  [the longest x1 9.79 us: local(): inner_weight[None]]
    ppermute x3 -> x0, starting transfers between devices: 8.92 us -> none  [partner(): lax.ppermute(array, axis, [(i, i ^ 1 << stride) for i in range(lax.axis_s...]
  transfers between devices with their start and end apart: 7 -> 0, of which waited for: 5 -> 0; matrix products, arithmetic and copies ran while one was open for 6% -> 0% of each run, Pallas kernels for 0% -> 0%
where the time goes in v1:
time: 107 us; the launch traced here: 106 us
  Pallas kernels  98.5 us (92%)
  local copies, waits for them, and re-layouts  5.07 us (5%)
  other arithmetic  1.29 us (1%)
    pallas_call x1, Pallas kernels, local(): pl.pallas_call(kernel, out_shape=(jax.ShapeDtypeStruct((64, COLS), BF16),...  98.5 us
    unnamed x5, local copies, waits for them, and re-layouts  5.07 us

profile of v1, /device:TPU:24, one launch (start us, length us, event | category | flops | bytes accessed | tf_op | source)
XLA Modules:
  0.0 105.5 jit_solution(3860356447550725250)
XLA Ops:
  0.6 1.3 %reshape.13 = f32[2048]{0:T(1024)} convert(bf16[2048]{0:T(1024)(128)(2,1)} %param.10) | non-fusion elementwise | flops 2048 | bytes 12288 | tf_op jit(solution)/shard_map/reshape | solution.py:427
  1.9 98.5 %shard_map.94 = (bf16[64,1024]{1,0:T(8,128)(2,1)}, bf16[896,1024]{1,0:T(8,128)(2,1)}, bf16[32,896]{1,0:T(8,128)(2,1)}) custom-call(bf16[256,896]{1,0:T(8,128)(2,1)} %h_hbm.1, bf16[64,1024]{1,0:T(8,128)(2,1)} %r_hbm.1, bf16[64,1024]{1,0:T(8,128)(2,1)} %c_hbm.1, f32[2,1,1024]{2,1,0:T(1,128)} %bitcast.7, bf16[896,1024]{1,0:T(8,128)(2,1)} %w_hbm.1, ...), custom_call_target="tpu_custom_call" | custom-call | tf_op jit(solution)/shard_map/pallas_call | solution.py:430
  100.5 1.6 %copy.13 = bf16[64,1024]{1,0:T(8,128)(2,1)} copy(bf16[64,1024]{1,0:T(8,128)(2,1)} %get-tuple-element.12) | data formatting | bytes 262144
  102.0 0.0 copy-start
  102.0 2.9 %copy.14 = bf16[896,1024]{1,0:T(8,128)(2,1)} copy(bf16[896,1024]{1,0:T(8,128)(2,1)} %get-tuple-element.13) | data formatting | bytes 3670016
  104.9 0.0 copy-done
  104.9 0.6 copy.15
Async XLA Ops:
  102.0 2.9 %copy-start = (bf16[32,896]{1,0:T(8,128)(2,1)S(1)}, bf16[32,896]{1,0:T(8,128)(2,1)}, u32[]{:S(2)}) copy-start(bf16[32,896]{1,0:T(8,128)(2,1)} %get-tuple-element.8) | copy-start | bytes 172036

commit v2 on v1

v2 whole, which is shorter than its diff:
```python
import math

import jax
import jax.numpy as jnp
from jax import lax
from jax.experimental import pallas as pl
from jax.experimental.pallas import tpu as pltpu
from jax.sharding import PartitionSpec as P

FF = 7168
TOK = 512

inner_rate = 0.2
outer_rate = 0.7
outer_mu = 0.9
mix_share = 0.5

F32 = jnp.float32
BF16 = jnp.bfloat16
ROWS = 896
COLS = 1024
CHUNKS = ((0, 256), (256, 256), (512, 256), (768, 128))
NCH = len(CHUNKS)
PIECES = 2
PIECE = 64 // PIECES
MIXCOLS = 256
VMEM_LIMIT = 28 * 1024 * 1024
REPLICAS = 32
FEATURES = 2048
MULT = 1.0 / math.sqrt(FF)
STEP = inner_rate * math.sqrt(FF / TOK)
NSEM = 160


def kernel(
    h_hbm, r_hbm, c_hbm, gain16, w_hbm, at_hbm, mt_hbm,
    normed_hbm, mout_hbm, ht_hbm, sb, nfull,
    wv, hb, ht, p32, pb, ap1, ap2, xown, zsend, zrecv, rv, cv, stat_out, stat_in, slope, nout, gain,
    p1buf, cbuf, yrecv, yown, tt, q1r, qs, near, far, atv, mtv, nown, mo, ta, na,
    send, recv, loc,
):
    ri = lax.axis_index("replica")
    ti = lax.axis_index("tensor")
    s = lax.rem(ri, 2)
    chip = lax.div(ri, 2)
    z = lax.rem(chip, 8)
    y = lax.div(chip, 8)
    zh = lax.div(ti, 4)
    x = lax.rem(ti, 4)
    q = lax.div(z, 4)
    p = lax.rem(z, 4)
    zfar = 4 * (1 - q) + p
    o = 1 - s
    sy = lax.div(y, 2)
    je = lax.rem(y, 2)
    jo = 1 - je
    yb = 2 * s + jo
    plus = lax.rem(yb - y + 4, 4) == 1
    hc = jnp.where(plus, 1, 0)
    hd = 1 - hc
    side = 1 - hc
    yo = lax.rem(2 * y - yb + 4, 4)
    yup = lax.rem(y + 1, 4)
    ydn = lax.rem(y + 3, 4)
    xup = lax.rem(x + 1, 4)
    xdn = lax.rem(x + 3, 4)
    xfar = lax.rem(x + 2, 4)
    own = s == sy
    is_near = s == q

    def dev(yy=y, zz=z, cc=s, hh=zh, xx=x):
        return ((yy * 8 + zz) * 2 + cc, hh * 4 + xx)

    ids = {}
    used = [0, 0]

    def sid(name, count=1):
        if name not in ids:
            kind = name[0][0] == "r"
            ids[name] = used[kind]
            used[kind] += count
            assert used[kind] <= NSEM
        return ids[name]

    pending = []

    def when(cond, f):
        if cond is None:
            f()
        else:
            pl.when(cond)(f)

    other = dev(cc=o)

    def go(sname, ridx, src, dst, device, cond=None):
        d = pltpu.make_async_remote_copy(
            src_ref=src, dst_ref=dst, send_sem=send.at[sid(("s",) + sname)], recv_sem=recv.at[ridx],
            device_id=device, device_id_type=pl.DeviceIdType.MESH,
        )
        when(cond, d.start)
        pending.append((cond, d))

    def got(ridx, dst, cond=None):
        d = pltpu.make_async_remote_copy(
            src_ref=dst, dst_ref=dst, send_sem=send.at[0], recv_sem=recv.at[ridx],
            device_id=other, device_id_type=pl.DeviceIdType.MESH,
        )
        when(cond, d.wait_recv)

    nloc = [0]

    def local_copy(src, dst):
        d = pltpu.make_async_copy(src, dst, loc.at[nloc[0]])
        nloc[0] += 1
        return d

    peers = [other, dev(xx=xup), dev(xx=xdn), dev(hh=1 - zh)]
    for yy in (yup, ydn):
        peers += [dev(yy=yy, cc=0), dev(yy=yy, cc=1)]
    for k in (1, 2, 3):
        peers.append(dev(zz=4 * q + lax.rem(p + k, 4)))
    peers += [dev(zz=zfar, cc=0), dev(zz=zfar, cc=1)]
    lw = local_copy(w_hbm, wv)
    lh = local_copy(h_hbm, hb.at[s])
    lr = local_copy(r_hbm, rv)
    lc = local_copy(c_hbm, cv)
    la = local_copy(at_hbm, atv)
    lm = local_copy(mt_hbm, mtv)
    for d in (lh, lw, lr, lc, la, lm):
        d.start()
    barrier = pltpu.get_barrier_semaphore()
    for peer in peers:
        pl.semaphore_signal(barrier, inc=1, device_id=peer, device_id_type=pl.DeviceIdType.MESH)

    def lane(value):
        return pl.multiple_of(value, 256)

    def wcols(j, h):
        return pl.ds(lane(j * 512 + h * 256), 256)

    def hidden_send():
        go(("h",), sid(("r_h",)), h_hbm, hb.at[s], other)

    own_local = {}

    def far_block(k):
        r0, n = CHUNKS[k]
        rows = pl.ds(r0, n)
        rp1 = sid(("r_p1", k))
        go(("p1a", k), rp1, w_hbm.at[rows, wcols(je, 0)], p1buf.at[rows], dev(yy=ydn), jnp.logical_not(own))
        go(("p1b", k), rp1, w_hbm.at[rows, wcols(je, 1)], p1buf.at[rows], dev(yy=yup), jnp.logical_not(own))
        go(("yo", k), sid(("r_yo", k)), w_hbm.at[rows, wcols(je, o)], yown.at[rows], other, own)
        d = local_copy(w_hbm.at[rows, wcols(je, s)], yown.at[rows])
        when(own, d.start)
        own_local[k] = d

    def direct_half(k):
        r0, n = CHUNKS[k]
        rows = pl.ds(r0, n)
        ryr = sid(("r_yr", k), 2)
        go(("yd", k), ryr + side, w_hbm.at[rows, wcols(jo, hd)], yrecv.at[side, rows], dev(yy=yb, cc=hd))

    def partial_out(half):
        @pl.loop(0, COLS // 256)
        def _(i):
            cols = pl.ds(lane(i * 256), 256)
            v = jnp.dot(hb[half], wv[:, cols], preferred_element_type=F32).reshape(4, 64, 256)
            p32[half, :, :, cols] = v
            pb[half, :, :, cols] = v.astype(BF16)

    def first_out():
        lh.wait()
        lw.wait()
        partial_out(s)

    def second_out():
        got(sid(("r_h",)), hb.at[o])
        partial_out(o)

    halves = (1 - zh, zh)

    def x_far(k, j):
        hf = halves[k]
        ra = sid(("r_ap1", k, j), 2)
        for h, target in ((0, xdn), (1, xup)):
            part = pl.ds(PIECE * j + h * (PIECE // 2), PIECE // 2)
            go(("ap1", k, j, h), ra + h, pb.at[hf, xfar, part], ap1.at[k, j, h], dev(xx=target))

    def combine(k):
        r0, n = CHUNKS[k]
        rows = pl.ds(r0, n)
        got(sid(("r_p1", k)), p1buf.at[rows])

        @pl.loop(0, n // 128)
        def _(i):
            t = pl.ds(pl.multiple_of(r0 + i * 128, 128), 128)
            cbuf[t, :] = (wv[t, wcols(jo, hc)].astype(F32) + p1buf[t, :].astype(F32)).astype(BF16)

        go(("yc", k), sid(("r_yr", k)) + side, cbuf.at[rows], yrecv.at[side, rows], dev(yy=yb, cc=hc))

    def x_near(k, j):
        hf = halves[k]
        ra = sid(("r_ap1", k, j))
        rb = sid(("r_ap2", k, j), 2)
        part = pl.ds(PIECE * j, PIECE)
        for h, target in ((1, xup), (0, xdn)):
            got(ra + h, ap1.at[k, j, h])
            r0 = PIECE * j + h * (PIECE // 2)
            r1 = r0 + PIECE // 2
            pb[hf, target, r0:r1, :] = (p32[hf, target, r0:r1, :] + ap1[k, j, h].astype(F32)).astype(BF16)
            go(("ap2", k, j, h), rb + 1 - h, pb.at[hf, target, part], ap2.at[k, j, 1 - h], dev(xx=target))

    def turn_hidden():
        for hf in range(2):
            @pl.loop(0, ROWS // 128)
            def _(i):
                t = pl.ds(pl.multiple_of(i * 128, 128), 128)
                ht[hf, t, :] = hb[hf, :, t].astype(F32).T.astype(BF16)
        lt.start()

    def quad_send(k):
        r0, n = CHUNKS[k]
        rows = pl.ds(r0, n)
        for i in range(2):
            got(sid(("r_yr", k)) + i, yrecv.at[i, rows])
        got(sid(("r_yo", k)), yown.at[rows], jnp.logical_not(own))
        when(own, own_local[k].wait)

        @pl.loop(0, n // 128)
        def _(i):
            t = pl.ds(pl.multiple_of(r0 + i * 128, 128), 128)
            v = yown[t, :].astype(F32) + yrecv[0, t, :].astype(F32) + yrecv[1, t, :].astype(F32)
            tt[:, :, t] = v.T.astype(BF16).reshape(4, 64, 128)

        rq = sid(("r_q", k), 3)
        for m in (1, 2, 3):
            pm = lax.rem(p + m, 4)
            go(("q", k, m), rq + m - 1, tt.at[pm, :, rows], q1r.at[m - 1, :, rows], dev(zz=4 * q + pm))

    def finish_out(k, j):
        hf = halves[k]
        rb = sid(("r_ap2", k, j))
        got(rb, ap2.at[k, j, 0])
        got(rb + 1, ap2.at[k, j, 1])
        v = p32[hf, x, PIECE * j:PIECE * (j + 1), :]
        return v + ap2[k, j, 0].astype(F32) + ap2[k, j, 1].astype(F32)

    def z_send(j):
        zsend[j] = finish_out(0, j).astype(BF16)
        go(("z", j), sid(("r_z", j)), zsend.at[j], zrecv.at[j], dev(hh=1 - zh))

    def x_own(j):
        xown[j] = finish_out(1, j)

    def far_send(k):
        r0, n = CHUNKS[k]
        rows = pl.ds(r0, n)
        rq = sid(("r_q", k))
        for m in (1, 2, 3):
            got(rq + m - 1, q1r.at[m - 1, :, rows])
        v = tt[p, :, r0:r0 + n].astype(F32)
        for m in range(3):
            v = v + q1r[m, :, r0:r0 + n].astype(F32)
        qs[:, :, r0:r0 + n] = v.astype(BF16).reshape(2, 32, n)
        rn = sid(("r_near", k))
        rf = sid(("r_far", k))
        go(("near", k), rn, qs.at[o, :, rows], near.at[:, rows], other, is_near)
        for c in range(2):
            go(("far", k, c), rf, qs.at[c, :, rows], far.at[:, rows], dev(zz=zfar, cc=c), jnp.logical_not(is_near))

        @pl.when(is_near)
        def _():
            near[:, r0:r0 + n] = qs[s, :, r0:r0 + n]

    def stats(j):
        if j == 0:
            lr.wait()
            lc.wait()
        part = slice(PIECE * j, PIECE * (j + 1))
        got(sid(("r_z", j)), zrecv.at[j])
        xin = rv[part, :].astype(F32) + (xown[j] + zrecv[j].astype(F32)) * MULT
        dz = cv[part, :].astype(F32) * gain[...]
        xown[j] = xin
        stat_out[j, 0] = jnp.broadcast_to(jnp.sum(xin * xin, axis=-1, keepdims=True), (PIECE, 128))
        stat_out[j, 1] = jnp.broadcast_to(jnp.sum(dz * xin, axis=-1, keepdims=True), (PIECE, 128))
        go(("stat", j), sid(("r_stat", j)), stat_out.at[j], stat_in.at[j], other)

    def norm(j):
        part = slice(PIECE * j, PIECE * (j + 1))
        rows = pl.ds(PIECE * j, PIECE)
        got(sid(("r_stat", j)), stat_in.at[j])
        mean_sq = (stat_out[j, 0, :, 0:1] + stat_in[j, 0, :, 0:1]) / FEATURES
        inner_mean = (stat_out[j, 1, :, 0:1] + stat_in[j, 1, :, 0:1]) / FEATURES
        root_inv = lax.rsqrt(mean_sq + 1e-05)
        xin = xown[j]
        dz = cv[part, :].astype(F32) * gain[...]
        slope[part, :] = (root_inv * (dz - xin * (inner_mean * root_inv * root_inv))).astype(BF16)
        go(("zs", j), sid(("r_zs", j)), slope.at[rows], sb.at[zh, x, rows], dev(hh=1 - zh))
        spread(0, j, slope.at[rows])
        nout[part, :] = (xin * root_inv * gain[...]).astype(BF16)
        if j == PIECES - 1:
            ln.start()
            ls.start()

    def spread(k, j, src):
        rs = sid(("r_s", k, j), 4)
        dst = sb.at[(zh, 1 - zh)[k], x, pl.ds(PIECE * j, PIECE)]
        go(("su", k, j), rs, src, dst, dev(xx=xup))
        go(("sd", k, j), rs + 1, src, dst, dev(xx=xdn))

    def relay(k, j):
        rs = sid(("r_s", k, j))
        hf = (zh, 1 - zh)[k]
        for h, source, target in ((1, xup, xdn), (0, xdn, xup)):
            got(rs + h, sb.at[hf, source, pl.ds(PIECE * j, PIECE)])
            part = sb.at[hf, source, pl.ds(PIECE * j + h * (PIECE // 2), PIECE // 2)]
            go(("f", k, j, h), rs + 2 + h, part, part, dev(xx=target))

    def relayed(k, j):
        rs = sid(("r_s", k, j))
        for h in range(2):
            got(rs + 2 + h, sb.at[(zh, 1 - zh)[k], xfar, pl.ds(PIECE * j + h * (PIECE // 2), PIECE // 2)])

    def update(k):
        if k == 0:
            la.wait()
            lm.wait()
        r0, n = CHUNKS[k]
        rows = pl.ds(r0, n)
        cut = slice(r0, r0 + n)
        got(sid(("r_near", k)), near.at[:, rows], jnp.logical_not(is_near))
        got(sid(("r_far", k)), far.at[:, rows])
        total = near[:, cut].astype(F32) + far[:, cut].astype(F32)
        anchor = atv[:, cut].astype(F32)
        pseudo = anchor - total / REPLICAS
        moment = (outer_mu * mtv[:, cut].astype(F32) + pseudo).astype(BF16)
        mo[:, cut] = moment
        fresh = (anchor - outer_rate * (pseudo + outer_mu * moment.astype(F32))).astype(BF16)
        nown[:, cut] = fresh
        rt = sid(("r_ta", k), 2)
        go(("tf", k), rt + s, nown.at[:, rows], ta.at[p, s, :, rows], dev(zz=zfar, cc=q))
        go(("tn", k), rt + s, nown.at[:, rows], ta.at[p, s, :, rows], other, jnp.logical_not(is_near))

        @pl.when(is_near)
        def _():
            ta[p, s, :, cut] = fresh

        if k == NCH - 1:
            lo.start()

    def quad_gather(k):
        r0, n = CHUNKS[k]
        rows = pl.ds(r0, n)
        rt = sid(("r_ta", k))
        for c in range(2):
            got(rt + c, ta.at[p, c, :, rows], jnp.logical_not(jnp.logical_and(is_near, s == c)))
        rg = sid(("r_g", k), 3)
        for m in (1, 2, 3):
            pm = lax.rem(p + m, 4)
            go(("g", k, m), rg + m - 1, ta.at[p, :, :, rows], ta.at[p, :, :, rows], dev(zz=4 * q + pm))

    def row_gather(k):
        r0, n = CHUNKS[k]
        rows = pl.ds(r0, n)
        rg = sid(("r_g", k))
        for m in (1, 2, 3):
            got(rg + m - 1, ta.at[lax.rem(p + 4 - m, 4), :, :, rows])

        @pl.loop(0, n // 128)
        def _(i):
            t = pl.ds(pl.multiple_of(r0 + i * 128, 128), 128)
            na[t, :] = ta[:, :, :, t].reshape(256, 128).astype(F32).T.astype(BF16)

        ro = sid(("r_no", k), 2)
        re = sid(("r_ne", k), 2)
        dst = nfull.at[rows, wcols(je, s)]
        go(("nu", k), ro + s, na.at[rows], dst, dev(yy=yup, cc=sy))
        go(("nd", k), ro + s, na.at[rows], dst, dev(yy=ydn, cc=sy))
        go(("nn", k), re + s, na.at[rows], dst, other, jnp.logical_not(own))
        d = local_copy(na.at[rows], dst)
        when(own, d.start)
        own_out.append(d)

    def z_spread(j):
        part = sb.at[1 - zh, x, pl.ds(PIECE * j, PIECE)]
        got(sid(("r_zs", j)), part)
        spread(1, j, part)

    def row_relay(k):
        r0, n = CHUNKS[k]
        rows = pl.ds(r0, n)
        ro = sid(("r_no", k))
        for h in range(2):
            got(ro + h, nfull.at[rows, wcols(jo, h)])
        part = nfull.at[rows, wcols(jo, hc)]
        go(("nf", k), sid(("r_ne", k)) + hc, part, part, dev(yy=yo))

    def row_done(k):
        r0, n = CHUNKS[k]
        re = sid(("r_ne", k))
        for h in range(2):
            got(re + h, nfull.at[pl.ds(r0, n), wcols(je, h)], jnp.logical_not(jnp.logical_and(own, s == h)))

    ln = local_copy(nout, normed_hbm)
    lo = local_copy(mo, mout_hbm)
    ls = local_copy(slope, sb.at[zh, x])
    lt = local_copy(ht, ht_hbm)
    own_out = []

    def enter():
        pl.semaphore_wait(barrier, len(peers))

    def gain_row():
        v = gain16[pl.ds(pl.multiple_of(8 * s, 8), 8), :].astype(F32)
        for i in range(8):
            gain[:, 128 * i:128 * (i + 1)] = v[i:i + 1, :]

    steps = (
        (first_out,), (gain_row,), (enter,), (hidden_send,), (far_block, 0), (direct_half, 0), (far_block, 1),
        (second_out,), (x_far, 0, 0), (x_far, 0, 1), (x_far, 1, 0), (x_far, 1, 1), (combine, 0), (direct_half, 1),
        (far_block, 2), (x_near, 0, 0), (x_near, 0, 1), (combine, 1), (direct_half, 2), (far_block, 3),
        (quad_send, 0), (x_near, 1, 0), (x_near, 1, 1), (combine, 2), (direct_half, 3), (z_send, 0), (z_send, 1),
        (combine, 3), (quad_send, 1), (far_send, 0), (x_own, 0), (x_own, 1), (quad_send, 2), (far_send, 1),
        (update, 0), (quad_send, 3), (far_send, 2), (update, 1), (quad_gather, 0), (turn_hidden,), (far_send, 3),
        (update, 2), (quad_gather, 1), (row_gather, 0), (stats, 0), (norm, 0), (stats, 1), (norm, 1), (update, 3),
        (quad_gather, 2), (row_gather, 1), (quad_gather, 3), (relay, 0, 0), (relay, 0, 1), (row_relay, 0),
        (row_gather, 2), (row_relay, 1), (z_spread, 0), (z_spread, 1), (row_gather, 3), (relayed, 0, 0),
        (relayed, 0, 1), (row_relay, 2), (relay, 1, 0), (relay, 1, 1), (row_relay, 3), (relayed, 1, 0),
        (relayed, 1, 1), (row_done, 0), (row_done, 1), (row_done, 2), (row_done, 3),
    )
    for step, *args in steps:
        step(*args)
    for cond, d in pending:
        when(cond, d.wait_send)
    for d in (ln, lo, ls, lt):
        d.wait()
    for d in own_out:
        when(own, d.wait)


def mix_kernel(ht, sb, w, n, normed_in, mout_in, mixed, normed_out, mout_out, sem):
    i = pl.program_id(0)
    shrink = mix_share * STEP * MULT
    copies = (
        pltpu.make_async_copy(normed_in, normed_out, sem.at[0]),
        pltpu.make_async_copy(mout_in, mout_out, sem.at[1]),
    )

    @pl.when(i == 0)
    def _():
        for d in copies:
            d.start()

    g = jnp.dot(ht[0], sb[0].reshape(256, MIXCOLS), preferred_element_type=F32)
    g = g + jnp.dot(ht[1], sb[1].reshape(256, MIXCOLS), preferred_element_type=F32)
    mixed[...] = (mix_share * w[...].astype(F32) - shrink * g + (1.0 - mix_share) * n[...].astype(F32)).astype(BF16)

    @pl.when(i == pl.num_programs(0) - 1)
    def _():
        for d in copies:
            d.wait()


def local(hidden_act, residual_in, cotangent, norm_gain, inner_weight, anchor, momentum):
    hbm = pl.BlockSpec(memory_space=pl.ANY)
    away = pl.BlockSpec(memory_space=pltpu.HBM)
    vmem = pl.BlockSpec(memory_space=pltpu.VMEM)
    b16 = lambda *shape: pltpu.VMEM(shape, BF16)
    f32 = lambda *shape: pltpu.VMEM(shape, F32)
    stay = lambda v: pltpu.with_memory_space_constraint(v, pltpu.HBM)
    like = lambda *shape: jax.ShapeDtypeStruct(shape, BF16)
    normed, moment, ht, sb, nfull = pl.pallas_call(
        kernel,
        out_shape=(like(64, COLS), like(32, ROWS), like(2, ROWS, 256), like(2, 4, 64, COLS), like(ROWS, COLS)),
        in_specs=[away, away, away, vmem, away, away, away],
        out_specs=(hbm,) * 5,
        scratch_shapes=[
            b16(ROWS, COLS), b16(2, 256, ROWS), b16(2, ROWS, 256), f32(2, 4, 64, COLS), b16(2, 4, 64, COLS),
            b16(2, PIECES, 2, PIECE // 2, COLS), b16(2, PIECES, 2, PIECE, COLS), f32(PIECES, PIECE, COLS),
            b16(PIECES, PIECE, COLS), b16(PIECES, PIECE, COLS), b16(64, COLS), b16(64, COLS),
            f32(PIECES, 2, PIECE, 128), f32(PIECES, 2, PIECE, 128), b16(64, COLS), b16(64, COLS), f32(1, COLS),
            b16(ROWS, 256), b16(ROWS, 256), b16(2, ROWS, 256), b16(ROWS, 256), b16(4, 64, ROWS),
            b16(3, 64, ROWS), b16(2, 32, ROWS), b16(32, ROWS), b16(32, ROWS), b16(32, ROWS), b16(32, ROWS),
            b16(32, ROWS), b16(32, ROWS), b16(4, 2, 32, ROWS), b16(ROWS, 256),
            pltpu.SemaphoreType.DMA((NSEM,)), pltpu.SemaphoreType.DMA((NSEM,)), pltpu.SemaphoreType.DMA((24,)),
        ],
        compiler_params=pltpu.CompilerParams(
            collective_id=0, has_side_effects=True, vmem_limit_bytes=VMEM_LIMIT
        ),
    )(
        stay(hidden_act), stay(residual_in), stay(cotangent), norm_gain.reshape(16, 128), stay(inner_weight),
        stay(anchor.T), stay(momentum.T),
    )
    column = lambda i: (0, i)
    mixed, normed, moment = pl.pallas_call(
        mix_kernel,
        grid=(COLS // MIXCOLS,),
        out_shape=(like(ROWS, COLS), like(64, COLS), like(32, ROWS)),
        in_specs=[
            pl.BlockSpec((2, ROWS, 256), lambda i: (0, 0, 0)),
            pl.BlockSpec((2, 4, 64, MIXCOLS), lambda i: (0, 0, 0, i)),
            pl.BlockSpec((ROWS, MIXCOLS), column),
            pl.BlockSpec((ROWS, MIXCOLS), column),
            hbm, hbm,
        ],
        out_specs=(pl.BlockSpec((ROWS, MIXCOLS), column), hbm, hbm),
        scratch_shapes=[pltpu.SemaphoreType.DMA((2,))],
        compiler_params=pltpu.CompilerParams(vmem_limit_bytes=24 * 1024 * 1024),
    )(ht, sb, inner_weight, nfull, normed, moment)
    return (normed, mixed, moment.T)


def solution(mesh):
    in_specs = (
        P("replica", "tensor"),
        P("tensor", "replica"),
        P("tensor", "replica"),
        P(),
        P("tensor", "replica"),
        P("tensor", "replica"),
        P("tensor", "replica"),
    )
    out_specs = (P("tensor", "replica"), P("tensor", "replica"), P("tensor", "replica"))
    return jax.shard_map(local, mesh=mesh, in_specs=in_specs, out_specs=out_specs, check_vma=False)
```

time: 107 us -> 95 us (0.89)
  the two profiles are of different devices: /device:TPU:24 before, /device:TPU:56 now
where the time goes in v2:
time: 95 us; the launch traced here: 94.9 us
  Pallas kernels  93.4 us (98%)
    pallas_call x1, Pallas kernels, local(): pl.pallas_call(kernel, out_shape=(like(64, COLS), like(32, ROWS), like(2,...  90.1 us
    pallas_call x1, Pallas kernels, local(): pl.pallas_call(mix_kernel, grid=(COLS // MIXCOLS,), out_shape=(like(ROWS,...  3.32 us

profile of v2, /device:TPU:56, one launch (start us, length us, event | category | flops | bytes accessed | tf_op | source)
XLA Modules:
  0.0 94.9 jit_solution(3483215019465186298)
XLA Ops:
  0.6 0.0 copy-start
  0.6 0.0 copy-start.1
  0.7 0.8 copy-done.1
  1.5 90.1 %shard_map.94 = (bf16[64,1024]{1,0:T(8,128)(2,1)S(1)}, bf16[32,896]{1,0:T(8,128)(2,1)S(1)}, bf16[2,896,256]{2,1,0:T(8,128)(2,1)S(1)}, bf16[2,4,64,1024]{3,2,1,0:T(8,128)(2,1)S(1)}, bf16[896,1024]{1,0:T(8,128)(2,1)S(1)}) custom-call(bf16[256,896]{1,0:T(8,128)(2,1)} %h_hbm.1, bf16[64,1024]{1,0:T(8,128)(2,1)} %r_hbm.1, bf16[64,1024]{1,0:T(8,128)(2,1)} %c_hbm.1, ...), custom_call_target="tpu_custom_call" | custom-call | tf_op jit(solution)/shard_map/pallas_call | solution.py:472
  91.5 0.0 copy-done
  91.6 3.3 %shard_map.95 = (bf16[896,1024]{1,0:T(8,128)(2,1)}, bf16[64,1024]{1,0:T(8,128)(2,1)}, bf16[32,896]{1,0:T(8,128)(2,1)}) custom-call(bf16[2,896,256]{2,1,0:T(8,128)(2,1)S(1)} %get-tuple-element.11.ht, bf16[2,4,64,1024]{3,2,1,0:T(8,128)(2,1)S(1)} %get-tuple-element.12.sb, bf16[896,1024]{1,0:T(8,128)(2,1)S(1)} %copy-done, ...), custom_call_target="tpu_custom_call" | custom-call | tf_op jit(solution)/shard_map/pallas_call | solution.py:495
Async XLA Ops:
  0.6 90.9 %copy-start = (bf16[896,1024]{1,0:T(8,128)(2,1)S(1)}, bf16[896,1024]{1,0:T(8,128)(2,1)}, u32[]{:S(2)}) copy-start(bf16[896,1024]{1,0:T(8,128)(2,1)} %w.1) | copy-start | bytes 5505028
  0.6 0.8 copy-start.1

commit v3 on v2

--- a/solution.py
+++ b/solution.py
@@ -416,14 +416,14 @@
             gain[:, 128 * i:128 * (i + 1)] = v[i:i + 1, :]
 
     steps = (
-        (first_out,), (gain_row,), (enter,), (hidden_send,), (far_block, 0), (direct_half, 0), (far_block, 1),
-        (second_out,), (x_far, 0, 0), (x_far, 0, 1), (x_far, 1, 0), (x_far, 1, 1), (combine, 0), (direct_half, 1),
-        (far_block, 2), (x_near, 0, 0), (x_near, 0, 1), (combine, 1), (direct_half, 2), (far_block, 3),
-        (quad_send, 0), (x_near, 1, 0), (x_near, 1, 1), (combine, 2), (direct_half, 3), (z_send, 0), (z_send, 1),
-        (combine, 3), (quad_send, 1), (far_send, 0), (x_own, 0), (x_own, 1), (quad_send, 2), (far_send, 1),
-        (update, 0), (quad_send, 3), (far_send, 2), (update, 1), (quad_gather, 0), (turn_hidden,), (far_send, 3),
-        (update, 2), (quad_gather, 1), (row_gather, 0), (stats, 0), (norm, 0), (stats, 1), (norm, 1), (update, 3),
-        (quad_gather, 2), (row_gather, 1), (quad_gather, 3), (relay, 0, 0), (relay, 0, 1), (row_relay, 0),
+        (first_out,), (gain_row,), (enter,), (hidden_send,), (far_block, 0), (direct_half, 0),
+        (far_block, 1), (second_out,), (x_far, 0, 0), (x_far, 0, 1), (x_far, 1, 0), (x_far, 1, 1), (combine, 0),
+        (direct_half, 1), (far_block, 2), (x_near, 0, 0), (x_near, 0, 1), (combine, 1), (direct_half, 2),
+        (far_block, 3), (quad_send, 0), (x_near, 1, 0), (x_near, 1, 1), (combine, 2), (direct_half, 3), (z_send, 0),
+        (z_send, 1), (combine, 3), (quad_send, 1), (far_send, 0), (x_own, 0), (x_own, 1), (quad_send, 2),
+        (far_send, 1), (update, 0), (quad_send, 3), (far_send, 2), (update, 1), (quad_gather, 0), (turn_hidden,),
+        (far_send, 3), (update, 2), (quad_gather, 1), (row_gather, 0), (stats, 0), (update, 3), (norm, 0), (stats, 1),
+        (quad_gather, 2), (norm, 1), (row_gather, 1), (quad_gather, 3), (relay, 0, 0), (relay, 0, 1), (row_relay, 0),
         (row_gather, 2), (row_relay, 1), (z_spread, 0), (z_spread, 1), (row_gather, 3), (relayed, 0, 0),
         (relayed, 0, 1), (row_relay, 2), (relay, 1, 0), (relay, 1, 1), (row_relay, 3), (relayed, 1, 0),
         (relayed, 1, 1), (row_done, 0), (row_done, 1), (row_done, 2), (row_done, 3),

time: 95 us -> 92.4 us (0.973)
  the two profiles are of different devices: /device:TPU:56 before, /device:TPU:32 now
where the time goes in v3:
time: 92.4 us; the launch traced here: 92.3 us
  Pallas kernels  90.8 us (98%)
    pallas_call x1, Pallas kernels, local(): pl.pallas_call(kernel, out_shape=(like(64, COLS), like(32, ROWS), like(2,...  87.5 us
    pallas_call x1, Pallas kernels, local(): pl.pallas_call(mix_kernel, grid=(COLS // MIXCOLS,), out_shape=(like(ROWS,...  3.32 us

profile of v3, /device:TPU:32, one launch (start us, length us, event | category | flops | bytes accessed | tf_op | source)
XLA Modules:
  0.0 92.3 jit_solution(9845799576575953888)
XLA Ops:
  0.6 0.0 copy-start
  0.6 0.0 copy-start.1
  0.7 0.8 copy-done.1
  1.5 87.5 %shard_map.94 = (bf16[64,1024]{1,0:T(8,128)(2,1)S(1)}, bf16[32,896]{1,0:T(8,128)(2,1)S(1)}, bf16[2,896,256]{2,1,0:T(8,128)(2,1)S(1)}, bf16[2,4,64,1024]{3,2,1,0:T(8,128)(2,1)S(1)}, bf16[896,1024]{1,0:T(8,128)(2,1)S(1)}) custom-call(bf16[256,896]{1,0:T(8,128)(2,1)} %h_hbm.1, bf16[64,1024]{1,0:T(8,128)(2,1)} %r_hbm.1, bf16[64,1024]{1,0:T(8,128)(2,1)} %c_hbm.1, ...), custom_call_target="tpu_custom_call" | custom-call | tf_op jit(solution)/shard_map/pallas_call | solution.py:472
  89.0 0.0 copy-done
  89.0 3.3 %shard_map.95 = (bf16[896,1024]{1,0:T(8,128)(2,1)}, bf16[64,1024]{1,0:T(8,128)(2,1)}, bf16[32,896]{1,0:T(8,128)(2,1)}) custom-call(bf16[2,896,256]{2,1,0:T(8,128)(2,1)S(1)} %get-tuple-element.11.ht, bf16[2,4,64,1024]{3,2,1,0:T(8,128)(2,1)S(1)} %get-tuple-element.12.sb, bf16[896,1024]{1,0:T(8,128)(2,1)S(1)} %copy-done, ...), custom_call_target="tpu_custom_call" | custom-call | tf_op jit(solution)/shard_map/pallas_call | solution.py:495
Async XLA Ops:
  0.6 88.3 %copy-start = (bf16[896,1024]{1,0:T(8,128)(2,1)S(1)}, bf16[896,1024]{1,0:T(8,128)(2,1)}, u32[]{:S(2)}) copy-start(bf16[896,1024]{1,0:T(8,128)(2,1)} %w.1) | copy-start | bytes 5505028
  0.6 0.8 copy-start.1
